TPU v7x, 32 devices: a whole 2x2x4 slice. The times are simulated.
32 devices in a mesh: groups: 2 (over x), tm: 16 (over z, y, core).
Axes of the slice: x: 2, y: 2, z: 4, core: 2. Of those that a mesh axis runs over, the one named last changes fastest.
Arguments:
- latent: bfloat16 [16384, 384], P(('groups', 'tm')), parts along dimension 0, may hold values from -45 to 45
- owner: int32 [16384], P(('groups', 'tm')), parts along dimension 0, may hold values from 0 to 15, as said below
- frame_counts: int32 [16], P('groups'), parts along dimension 0, may hold values from 1 to 8, 32 in all
- norm_gain: float32 [384], replicated, may hold values from 0.1 to 1.9
- norm_shift: float32 [384], replicated, may hold values from -3 to 3
- res_kernel: bfloat16 [3, 3, 3, 384, 384], replicated, may hold values from -0.0625 to 0.0625
- res_bias: float32 [384], replicated, may hold values from -3 to 3
- time_kernel: bfloat16 [3, 384, 768], replicated, may hold values from -0.1875 to 0.1875
- time_bias: float32 [768], replicated, may hold values from -3 to 3
- up_kernel: bfloat16 [3, 3, 384, 192], replicated, may hold values from -0.109375 to 0.109375
- up_bias: float32 [192], replicated, may hold values from -3 to 3
Outputs:
- frames_out: bfloat16 [128, 32, 6144], P(('groups', 'tm')), parts along dimension 0
There are 2 independent parts, one for each index of `groups`. A program takes and returns all parts, laid end to end along the dimension named above; an argument that names none is the same for every part. Nothing has to cross between parts.
Inputs may be any that keep to these rules, and one draw needn't show every extreme that they name: Each device's block of 512 tokens holds at most 64 tokens for any one owner, some block holds exactly 64 for one owner, and every device is the owner of exactly 512 tokens.
All inputs are finite; a program needn't handle non-finite values.
Results may differ from a plain program's by a relative error of at most 0.0057.
Values may be sent and summed in bfloat16 or wider, within the bound.
A program may use at most 128 MiB of HBM per device.

v0:
```python
import functools
import math

import jax
import jax.numpy as jnp
from jax import lax
from jax.experimental import pallas as pl
from jax.experimental.pallas import tpu as pltpu
from jax.sharding import PartitionSpec as P

H = 16
W = 16
PIXELS = H * W
FRAMES_HERE = 2
MESH = pl.DeviceIdType.MESH

epsilon = 1e-06


def kernel(
    n,
    owner_ref,
    counts_ref,
    latent_ref,
    gain_ref,
    shift_ref,
    res_bias_ref,
    time_bias_ref,
    up_bias_ref,
    res_hbm,
    time_hbm,
    up_hbm,
    out_ref,
    res_w,
    time_w,
    up_raw,
    up_w,
    packed_a,
    packed_b,
    recv_a,
    recv_b,
    order,
    meta_out,
    meta_in,
    acc,
    act_own_a,
    act_own_b,
    act_halo_a,
    act_halo_b,
    resid_own,
    resid_halo,
    windows_a,
    windows_b,
    temporal,
    enlarged,
    woven,
    pad_w,
    bias_row,
    load_sem,
    send_sem,
    recv_sem,
    meta_send_sem,
    meta_recv_sem,
    halo_send_sem,
    halo_recv_sem,
):
    me = lax.axis_index("tm")
    tokens, channels = latent_ref.shape
    capacity = packed_a.shape[1]
    packed, recv = (packed_a, packed_b), (recv_a, recv_b)
    act_own, act_halo = (act_own_a, act_own_b), (act_halo_a, act_halo_b)
    windows = (windows_a, windows_b)
    cut = packed_a.shape[2]
    spans = ((0, cut), (cut, channels))
    slots = n * capacity
    up_channels = up_raw.shape[2]
    wide = pad_w.shape[0]
    f32, bf16 = jnp.float32, jnp.bfloat16

    barrier = pltpu.get_barrier_semaphore()

    @pl.loop(1, n)
    def _(k):
        pl.semaphore_signal(
            barrier, inc=1, device_id={"tm": lax.rem(me + k, n)}, device_id_type=MESH
        )

    loads = [
        pltpu.make_async_copy(src, dst, load_sem.at[i])
        for i, (src, dst) in enumerate(((up_hbm, up_raw), (res_hbm, res_w), (time_hbm, time_w)))
    ]
    for load in loads:
        load.start()

    owner = owner_ref[...]
    relative = lax.rem(owner - me + n, n)
    peers = lax.broadcasted_iota(jnp.int32, (n, tokens), 0)
    marked = (relative == peers).astype(f32)
    earlier = (
        lax.broadcasted_iota(jnp.int32, (tokens, tokens), 0)
        < lax.broadcasted_iota(jnp.int32, (tokens, tokens), 1)
    ).astype(f32).astype(bf16)
    before = jnp.dot(marked.astype(bf16), earlier, preferred_element_type=f32)
    rank = jnp.sum(before * marked, 0, keepdims=True).astype(jnp.int32)
    position = relative * capacity + rank
    tally = jnp.sum(marked, 1, keepdims=True)

    per_group = 128 // capacity
    squares = latent_ref[...].astype(f32)
    squares = jnp.mean(squares * squares, -1, keepdims=True)
    scales = jnp.broadcast_to(lax.rsqrt(squares + epsilon), (tokens, 128)).T[0:1]
    lane = lax.rem(me, per_group) * capacity + rank
    lanes = lax.broadcasted_iota(jnp.int32, (128, tokens), 0)
    in_lane = (lanes == lane).astype(f32).astype(bf16)
    rest, scale_rows = scales, None
    for _ in range(3):
        piece = rest.astype(bf16).astype(f32)
        rest = rest - piece
        term = lax.dot_general(
            (marked * piece).astype(bf16),
            in_lane,
            (((1,), (1,)), ((), ())),
            preferred_element_type=f32,
        )
        scale_rows = term if scale_rows is None else scale_rows + term
    meta_row = lax.broadcasted_iota(jnp.int32, meta_out.shape, 1)
    meta_out[...] = jnp.where(meta_row == 0, tally[:, :, None], scale_rows[:, None, :])
    part = min(slots, 256)
    for c in range(slots // part):
        rows = lax.broadcasted_iota(jnp.int32, (part, tokens), 0) + c * part
        chosen = (rows == position).astype(f32).astype(bf16)
        block = jnp.dot(chosen, latent_ref[...], preferred_element_type=f32)
        per = part // capacity
        for i, (lo, hi) in enumerate(spans):
            packed[i][c * per : (c + 1) * per] = (
                block[:, lo:hi].reshape(per, capacity, hi - lo).astype(bf16)
            )

    pl.semaphore_wait(barrier, n - 1)

    @pl.loop(1, n)
    def _(k):
        peer = lax.rem(me + k, n)
        pltpu.make_async_remote_copy(
            src_ref=meta_out.at[k],
            dst_ref=meta_in.at[me],
            send_sem=meta_send_sem,
            recv_sem=meta_recv_sem,
            device_id={"tm": peer},
            device_id_type=MESH,
        ).start()

    for i in range(2):

        @pl.loop(1, n)
        def _(k):
            pltpu.make_async_remote_copy(
                src_ref=packed[i].at[k],
                dst_ref=recv[i].at[me],
                send_sem=send_sem.at[i],
                recv_sem=recv_sem.at[i],
                device_id={"tm": lax.rem(me + k, n)},
                device_id_type=MESH,
            ).start()

    meta_in[me] = meta_out[0]
    for i in range(2):
        recv[i][me] = packed[i][0]

    border = jnp.zeros((H, 3 * channels), bf16)
    for i, (lo, hi) in enumerate(spans):
        for j in range(3):
            for f in range(FRAMES_HERE):
                windows[i][j, f, 0:H] = border[:, : 3 * (hi - lo)]
                windows[i][j, f, H + PIXELS : 2 * H + PIXELS] = border[:, : 3 * (hi - lo)]
    for e in range(2 * FRAMES_HERE):
        enlarged[e, 0:H] = border
        enlarged[e, H + PIXELS : 2 * H + PIXELS] = border

    @pl.when(me == 0)
    def _():
        act_halo_a[...] = jnp.zeros_like(act_halo_a)
        act_halo_b[...] = jnp.zeros_like(act_halo_b)
        resid_halo[...] = jnp.zeros_like(resid_halo)

    pad_w[...] = jnp.zeros_like(pad_w)
    bias_row[...] = jnp.zeros_like(bias_row)
    bias_row[0:1, 0:up_channels] = up_bias_ref[...][None, :]
    loads[0].wait()
    folds = (((0,), (1, 2)), ((0, 1), (2,)))
    for q in range(2):
        lead = q * (wide - up_channels)
        if q == 1:
            pad_w[0:lead] = jnp.zeros((lead, channels), f32)
        for p in range(2):
            for i in range(2):
                for r in range(2):
                    total = None
                    for a in folds[p][i]:
                        for b in folds[q][r]:
                            term = up_raw[a, b].astype(f32)
                            total = term if total is None else total + term
                    pad_w[lead : lead + up_channels] = total
                    up_w[p, q, r, i * channels : (i + 1) * channels] = pad_w[...].T.astype(bf16)

    first = me * FRAMES_HERE
    keep = []
    for f in range(FRAMES_HERE):
        start = jnp.int32(0)
        begin = jnp.int32(0)
        for v in range(counts_ref.shape[0]):
            start = jnp.where(begin <= first + f, begin, start)
            begin = begin + counts_ref[v]
        keep.append(
            [jnp.where(first + f - 2 + j >= start, 1.0, 0.0).astype(f32) for j in range(2)]
        )

    def wait_all(src, dst, s_sem, r_sem):
        both = pltpu.make_async_remote_copy(
            src_ref=src.at[pl.ds(0, n - 1)],
            dst_ref=dst.at[pl.ds(0, n - 1)],
            send_sem=s_sem,
            recv_sem=r_sem,
            device_id={"tm": lax.rem(me + 1, n)},
            device_id_type=MESH,
        )
        both.wait_recv()
        both.wait_send()

    wait_all(meta_out, meta_in, meta_send_sem, meta_recv_sem)
    given = meta_in[:, 0, 0:1]
    slot = lax.broadcasted_iota(jnp.int32, (n, slots), 1)
    source = lax.broadcasted_iota(jnp.int32, (n, slots), 0)
    of_slot = slot // capacity
    here = jnp.sum(jnp.where(of_slot == source, given, 0.0), 0, keepdims=True).astype(jnp.int32)
    ahead = jnp.sum(jnp.where(source < of_slot, given, 0.0), 0, keepdims=True).astype(jnp.int32)
    row = lax.rem(slot[0:1], capacity)
    place = ahead + row
    pixel = lax.rem(place, PIXELS)
    place = place - pixel + lax.rem(pixel, W) * H + pixel // W
    place = jnp.where(row < here, place, -1)

    scale_of = jnp.concatenate(
        [
            jnp.sum(meta_in[g * per_group : (g + 1) * per_group, 1, :], 0, keepdims=True)
            for g in range(slots // 128)
        ],
        1,
    )
    row_scale = []
    for f in range(FRAMES_HERE):
        rows = lax.broadcasted_iota(jnp.int32, (PIXELS, slots), 0) + f * PIXELS
        chosen = rows == place
        order[f] = chosen.astype(f32).astype(bf16)
        row_scale.append(jnp.sum(jnp.where(chosen, scale_of, 0.0), 1, keepdims=True))
        acc[f] = jnp.broadcast_to(res_bias_ref[...][None, :], (PIXELS, channels))

    gain, shift = gain_ref[...][None, :], shift_ref[...][None, :]

    def shifted(value):
        y_index = lax.rem(lax.broadcasted_iota(jnp.int32, value.shape, 0), H)
        above = jnp.where(y_index == 0, 0.0, pltpu.roll(value, 1, 0))
        below = jnp.where(y_index == H - 1, 0.0, pltpu.roll(value, PIXELS - 1, 0))
        return above, value, below

    def store_shifted(target, three, scale=None):
        for a in range(3):
            value = three[a] if scale is None else three[a] * scale
            width = value.shape[1]
            target[H : H + PIXELS, a * width : (a + 1) * width] = value.astype(bf16)

    right = lax.rem(me + 1, n)

    def pass_on(i, own, halo):
        return pltpu.make_async_remote_copy(
            src_ref=own,
            dst_ref=halo,
            send_sem=halo_send_sem.at[i],
            recv_sem=halo_recv_sem.at[i],
            device_id={"tm": right},
            device_id_type=MESH,
        )

    def send(i, own, halo):
        @pl.when(me < n - 1)
        def _():
            pass_on(i, own, halo).start()

    def receive(i, own, halo):
        @pl.when(me > 0)
        def _():
            pass_on(i, own, halo).wait_recv()

    def sent(i, own, halo):
        @pl.when(me < n - 1)
        def _():
            pass_on(i, own, halo).wait_send()

    def land(i):
        lo, hi = spans[i]
        wait_all(packed[i], recv[i], send_sem.at[i], recv_sem.at[i])
        if capacity % 16:
            arrived = recv[i][...].astype(f32).reshape(slots, hi - lo).astype(bf16)
        else:
            arrived = recv[i][...].reshape(slots, hi - lo)
        for f in range(FRAMES_HERE):
            values = jnp.dot(order[f], arrived, preferred_element_type=f32)
            u = values * row_scale[f] * gain[:, lo:hi] + shift[:, lo:hi]
            act_own[i][f] = (u / (1.0 + jnp.exp(-u))).astype(bf16)
            acc[f, :, lo:hi] += values
        send(i, act_own[i], act_halo[i])
        for f in range(FRAMES_HERE):
            three = shifted(act_own[i][f].astype(f32))
            store_shifted(windows[i].at[2, f], three)
            if f == 0:
                store_shifted(windows[i].at[1, 1], three, keep[1][1])

    def land_halo(i):
        receive(i, act_own[i], act_halo[i])
        store_shifted(windows[i].at[0, 0], shifted(act_halo[i][0].astype(f32)), keep[0][0])
        three = shifted(act_halo[i][1].astype(f32))
        store_shifted(windows[i].at[1, 0], three, keep[0][1])
        store_shifted(windows[i].at[0, 1], three, keep[1][0])

    def convolve(i, j):
        lo, hi = spans[i]

        @pl.loop(0, 3)
        def _(b):
            weights = jnp.concatenate([res_w[j, a, b, lo:hi] for a in range(3)], 0)
            lhs = windows[i][j, :, pl.ds(pl.multiple_of(b * H, H), PIXELS), :]
            acc[...] += jnp.dot(
                lhs.reshape(FRAMES_HERE * PIXELS, 3 * (hi - lo)),
                weights,
                preferred_element_type=f32,
            ).reshape(FRAMES_HERE, PIXELS, channels)

    loads[1].wait()
    land(0)
    convolve(0, 2)
    land(1)
    land_halo(0)
    convolve(0, 1)
    convolve(0, 0)
    convolve(1, 2)
    land_halo(1)
    convolve(1, 1)
    convolve(1, 0)

    resid_own[...] = acc[...].astype(bf16)
    send(2, resid_own, resid_halo)
    loads[2].wait()
    temporal[...] = (
        jnp.dot(
            resid_own[...].reshape(FRAMES_HERE * PIXELS, channels),
            time_w[2],
            preferred_element_type=f32,
        ).reshape(temporal.shape)
        + time_bias_ref[...][None, None, :]
    )
    temporal[1] += keep[1][1] * jnp.dot(resid_own[0], time_w[1], preferred_element_type=f32)
    receive(2, resid_own, resid_halo)
    temporal[0] += keep[0][0] * jnp.dot(
        resid_halo[0], time_w[0], preferred_element_type=f32
    ) + keep[0][1] * jnp.dot(resid_halo[1], time_w[1], preferred_element_type=f32)
    temporal[1] += keep[1][0] * jnp.dot(resid_halo[1], time_w[0], preferred_element_type=f32)

    for e in range(2 * FRAMES_HERE):
        half = (e % 2) * channels
        frame = temporal[e // 2, :, half : half + channels].astype(bf16).astype(f32)
        store_shifted(enlarged.at[e], shifted(frame))

    shared = 2 * wide - 2 * up_channels

    def join(left, right):
        return (
            left[:, : wide - shared],
            left[:, wide - shared :] + right[:, :shared],
            right[:, shared:],
        )

    bias_left = bias_row[...]
    up_bias = [b[0:1] for b in join(bias_left, pltpu.roll(bias_left, wide - up_channels, 1))]

    @pl.loop(0, 2 * FRAMES_HERE)
    def _(e):
        for p in range(2):
            lanes = slice(p * channels, (p + 2) * channels)
            pieces = []
            for q in range(2):
                pieces.append(
                    jnp.dot(
                        enlarged[e, q * H : q * H + PIXELS, lanes],
                        up_w[p, q, 0],
                        preferred_element_type=f32,
                    )
                    + jnp.dot(
                        enlarged[e, (q + 1) * H : (q + 1) * H + PIXELS, lanes],
                        up_w[p, q, 1],
                        preferred_element_type=f32,
                    )
                )
            for i, piece in enumerate(join(*pieces)):
                woven[i, pl.ds(p, PIXELS, stride=2), :] = piece + up_bias[i]
        for i in range(3):
            value = woven[i].astype(bf16)
            for x in range(W):
                base = x * 2 * up_channels + i * woven.shape[2]
                out_ref[e, :, base : base + woven.shape[2]] = value[x * 2 * H : (x + 1) * 2 * H]

    for i in range(2):
        sent(i, act_own[i], act_halo[i])
    sent(2, resid_own, resid_halo)


def on_device(
    latent,
    owner,
    frame_counts,
    norm_gain,
    norm_shift,
    res_kernel,
    res_bias,
    time_kernel,
    time_bias,
    up_kernel,
    up_bias,
):
    n = lax.axis_size("tm")
    tokens, channels = latent.shape
    capacity = 2 * tokens // n
    up_channels = up_kernel.shape[-1]
    wide = 256
    cut = channels - 128
    f32, bf16 = jnp.float32, jnp.bfloat16
    vmem = pl.BlockSpec(memory_space=pltpu.VMEM)
    smem = pl.BlockSpec(memory_space=pltpu.SMEM)
    hbm = pl.BlockSpec(memory_space=pl.ANY)
    frame = (FRAMES_HERE, PIXELS)
    return pl.pallas_call(
        functools.partial(kernel, n),
        out_shape=pltpu.VMEM((2 * FRAMES_HERE, 2 * H, 2 * W * up_channels), bf16),
        in_specs=[vmem, smem, vmem, vmem, vmem, vmem, vmem, vmem, hbm, hbm, hbm],
        out_specs=vmem,
        scratch_shapes=[
            pltpu.VMEM(res_kernel.shape, bf16),
            pltpu.VMEM(time_kernel.shape, bf16),
            pltpu.VMEM((3, 3, up_channels, channels), bf16),
            pltpu.VMEM((2, 2, 2, 2 * channels, wide), bf16),
            pltpu.VMEM((n, capacity, cut), bf16),
            pltpu.VMEM((n, capacity, channels - cut), bf16),
            pltpu.VMEM((n, capacity, cut), bf16),
            pltpu.VMEM((n, capacity, channels - cut), bf16),
            pltpu.VMEM((*frame, n * capacity), bf16),
            pltpu.VMEM((n, 8, 128), f32),
            pltpu.VMEM((n, 8, 128), f32),
            pltpu.VMEM((*frame, channels), f32),
            pltpu.VMEM((*frame, cut), bf16),
            pltpu.VMEM((*frame, channels - cut), bf16),
            pltpu.VMEM((*frame, cut), bf16),
            pltpu.VMEM((*frame, channels - cut), bf16),
            pltpu.VMEM((*frame, channels), bf16),
            pltpu.VMEM((*frame, channels), bf16),
            pltpu.VMEM((3, FRAMES_HERE, PIXELS + 2 * H, 3 * cut), bf16),
            pltpu.VMEM((3, FRAMES_HERE, PIXELS + 2 * H, 3 * (channels - cut)), bf16),
            pltpu.VMEM((*frame, 2 * channels), f32),
            pltpu.VMEM((2 * FRAMES_HERE, PIXELS + 2 * H, 3 * channels), bf16),
            pltpu.VMEM((3, 2 * PIXELS, 2 * up_channels // 3), f32),
            pltpu.VMEM((wide, channels), f32),
            pltpu.VMEM((8, wide), f32),
            pltpu.SemaphoreType.DMA((3,)),
            pltpu.SemaphoreType.DMA((2,)),
            pltpu.SemaphoreType.DMA((2,)),
            pltpu.SemaphoreType.DMA,
            pltpu.SemaphoreType.DMA,
            pltpu.SemaphoreType.DMA((3,)),
            pltpu.SemaphoreType.DMA((3,)),
        ],
        compiler_params=pltpu.CompilerParams(
            collective_id=0, has_side_effects=True, vmem_limit_bytes=60 << 20
        ),
    )(
        owner.reshape(1, tokens),
        frame_counts,
        latent,
        norm_gain,
        norm_shift,
        res_bias,
        time_bias,
        up_bias,
        res_kernel,
        time_kernel,
        up_kernel.swapaxes(2, 3),
    )


def solution(mesh):
    placed = (
        P(("groups", "tm"), None),
        P(("groups", "tm")),
        P("groups"),
        P(),
        P(),
        P(),
        P(),
        P(),
        P(),
        P(),
        P(),
    )
    return jax.shard_map(
        on_device,
        mesh=mesh,
        in_specs=placed,
        out_specs=P(("groups", "tm"), None, None),
        check_vma=False,
    )
```

profile of v0, /device:TPU:16, one launch (start us, length us, event | category | flops | bytes accessed | tf_op | source)
XLA Modules:
  0.0 45.5 jit_solution(14364386725001573690)
XLA Ops:
  0.0 44.3 %shard_map.109 = bf16[4,32,6144]{2,1,0:T(8,128)(2,1)S(1)} custom-call(s32[1,512]{1,0:T(1,128)} %bitcast.3, s32[8]{0:T(128)} %counts_ref.1, bf16[512,384]{1,0:T(8,128)(2,1)} %latent_ref.1, f32[384]{0:T(512)} %gain_ref.1, f32[384]{0:T(512)} %shift_ref.1, f32[384]{0:T(512)} %res_bias_ref.1, f32[768]{0:T(1024)} %time_bias_ref.1, f32[192]{0:T(256)} %up_bias_ref.1, ...), custom_call_target="tpu_custom_call" | custom-call | tf_op jit(solution)/shard_map/pallas_call | solution.py:440
  44.3 1.1 %copy.13 = bf16[4,32,6144]{2,1,0:T(8,128)(2,1)} copy(bf16[4,32,6144]{2,1,0:T(8,128)(2,1)S(1)} %shard_map.109) | data formatting | bytes 3145728
where the time goes:
time: 45.6 us; the launch traced here: 45.5 us
  Pallas kernels  44.3 us (97%)
  local copies, waits for them, and re-layouts  1.15 us (3%)
    pallas_call x1, Pallas kernels, on_device(): pl.pallas_call(functools.partial(kernel, n), out_shape=pltpu.VMEM((2 * FR...  44.3 us
    unnamed x1, local copies, waits for them, and re-layouts  1.15 us

commit v1 on v0

v1 whole, which is shorter than its diff:
```python
import functools
import math

import jax
import jax.numpy as jnp
from jax import lax
from jax.experimental import pallas as pl
from jax.experimental.pallas import tpu as pltpu
from jax.sharding import PartitionSpec as P

H = 16
W = 16
PIXELS = H * W
FRAMES_HERE = 2
MESH = pl.DeviceIdType.MESH

epsilon = 1e-06


def kernel(
    n,
    owner_ref,
    counts_ref,
    latent_ref,
    gain_ref,
    shift_ref,
    res_bias_ref,
    time_bias_ref,
    up_bias_ref,
    res_hbm,
    time_hbm,
    up_hbm,
    out_ref,
    res_w,
    time_w,
    up_raw,
    up_w,
    packed,
    recv,
    order,
    meta_out,
    meta_in,
    acc,
    pass_out,
    pass_in,
    resid_own,
    resid_halo,
    windows,
    temporal,
    enlarged,
    woven,
    stack_w,
    bias_row,
    load_sem,
    send_sem,
    recv_sem,
    meta_send_sem,
    meta_recv_sem,
    halo_send_sem,
    halo_recv_sem,
):
    me = lax.axis_index("tm")
    tokens, channels = latent_ref.shape
    chunks, _, capacity, cut = packed.shape
    slots = n * capacity
    up_channels = up_raw.shape[2]
    pair = 2 * up_channels
    f32, bf16 = jnp.float32, jnp.bfloat16

    barrier = pltpu.get_barrier_semaphore()

    @pl.loop(1, n)
    def _(k):
        pl.semaphore_signal(
            barrier, inc=1, device_id={"tm": lax.rem(me + k, n)}, device_id_type=MESH
        )

    loads = [
        pltpu.make_async_copy(src, dst, load_sem.at[i])
        for i, (src, dst) in enumerate(((up_hbm, up_raw), (res_hbm, res_w), (time_hbm, time_w)))
    ]
    for load in loads:
        load.start()

    owner = owner_ref[...]
    relative = lax.rem(owner - me + n, n)
    peers = lax.broadcasted_iota(jnp.int32, (n, tokens), 0)
    marked = (relative == peers).astype(f32)
    earlier = (
        lax.broadcasted_iota(jnp.int32, (tokens, tokens), 0)
        < lax.broadcasted_iota(jnp.int32, (tokens, tokens), 1)
    ).astype(f32).astype(bf16)
    before = jnp.dot(marked.astype(bf16), earlier, preferred_element_type=f32)
    rank = jnp.sum(before * marked, 0, keepdims=True).astype(jnp.int32)
    position = relative * capacity + rank

    per_group = 128 // capacity
    squares = latent_ref[...].astype(f32)
    squares = jnp.mean(squares * squares, -1, keepdims=True)
    scales = jnp.broadcast_to(lax.rsqrt(squares + epsilon), (tokens, 128)).T[0:1]
    lane = lax.rem(me, per_group) * capacity + rank
    lanes = lax.broadcasted_iota(jnp.int32, (128, tokens), 0)
    in_lane = (lanes == lane).astype(f32).astype(bf16)
    rest, scale_rows = scales, None
    for _ in range(3):
        piece = rest.astype(bf16).astype(f32)
        rest = rest - piece
        term = lax.dot_general(
            (marked * piece).astype(bf16),
            in_lane,
            (((1,), (1,)), ((), ())),
            preferred_element_type=f32,
        )
        scale_rows = term if scale_rows is None else scale_rows + term
    meta_out[...] = scale_rows[:, None, :]
    part = min(slots, 256)
    for c in range(slots // part):
        rows = lax.broadcasted_iota(jnp.int32, (part, tokens), 0) + c * part
        chosen = (rows == position).astype(f32).astype(bf16)
        block = jnp.dot(chosen, latent_ref[...], preferred_element_type=f32)
        per = part // capacity
        for i in range(chunks):
            packed[i, c * per : (c + 1) * per] = (
                block[:, i * cut : (i + 1) * cut].reshape(per, capacity, cut).astype(bf16)
            )

    pl.semaphore_wait(barrier, n - 1)

    @pl.loop(1, n)
    def _(k):
        peer = lax.rem(me + k, n)
        pltpu.make_async_remote_copy(
            src_ref=meta_out.at[k],
            dst_ref=meta_in.at[me],
            send_sem=meta_send_sem,
            recv_sem=meta_recv_sem,
            device_id={"tm": peer},
            device_id_type=MESH,
        ).start()

    for i in range(chunks):

        @pl.loop(1, n)
        def _(k):
            pltpu.make_async_remote_copy(
                src_ref=packed.at[i, k],
                dst_ref=recv.at[i, me],
                send_sem=send_sem.at[i],
                recv_sem=recv_sem.at[i],
                device_id={"tm": lax.rem(me + k, n)},
                device_id_type=MESH,
            ).start()

    meta_in[me] = meta_out[0]
    for i in range(chunks):
        recv[i, me] = packed[i, 0]

    border = jnp.zeros((H, 3 * cut), bf16)
    for i in range(chunks):
        for f in range(FRAMES_HERE):
            windows[i, f, 0:H] = border
            windows[i, f, H + PIXELS : 2 * H + PIXELS] = border

    @pl.when(me == 0)
    def _():
        pass_in[...] = jnp.zeros_like(pass_in)
        resid_halo[...] = jnp.zeros_like(resid_halo)

    bias_row[...] = jnp.zeros_like(bias_row)
    bias_row[0:1, 0:up_channels] = up_bias_ref[...][None, :]
    loads[0].wait()
    folds = (((0,), (1, 2)), ((0, 1), (2,)))
    columns = ((1, 2), (0, 1), (0,), (2,))
    for p in range(2):
        for i in range(2):
            for r, taps in enumerate(columns):
                total = None
                for a in folds[p][i]:
                    for b in taps:
                        term = up_raw[a, b].astype(f32)
                        total = term if total is None else total + term
                stack_w[r * up_channels : (r + 1) * up_channels] = total
            for t in range(2 * pair // 128):
                up_w[p, i * channels : (i + 1) * channels, t * 128 : (t + 1) * 128] = (
                    stack_w[t * 128 : (t + 1) * 128].T.astype(bf16)
                )

    first = me * FRAMES_HERE
    keep = []
    for f in range(2 * FRAMES_HERE):
        start = jnp.int32(0)
        begin = jnp.int32(0)
        for v in range(counts_ref.shape[0]):
            start = jnp.where(begin <= first + f, begin, start)
            begin = begin + counts_ref[v]
        keep.append(
            [jnp.where(first + f - 2 + j >= start, 1.0, 0.0).astype(f32) for j in range(2)]
        )

    def wait_all(src, dst, s_sem, r_sem):
        both = pltpu.make_async_remote_copy(
            src_ref=src.at[pl.ds(0, n - 1)],
            dst_ref=dst.at[pl.ds(0, n - 1)],
            send_sem=s_sem,
            recv_sem=r_sem,
            device_id={"tm": lax.rem(me + 1, n)},
            device_id_type=MESH,
        )
        both.wait_recv()
        both.wait_send()

    wait_all(meta_out, meta_in, meta_send_sem, meta_recv_sem)
    given = jnp.sum(jnp.where(meta_in[:, 0, :] > 0.0, 1.0, 0.0), 1, keepdims=True)
    slot = lax.broadcasted_iota(jnp.int32, (n, slots), 1)
    source = lax.broadcasted_iota(jnp.int32, (n, slots), 0)
    of_slot = slot // capacity
    here = jnp.sum(jnp.where(of_slot == source, given, 0.0), 0, keepdims=True).astype(jnp.int32)
    ahead = jnp.sum(jnp.where(source < of_slot, given, 0.0), 0, keepdims=True).astype(jnp.int32)
    row = lax.rem(slot[0:1], capacity)
    place = ahead + row
    pixel = lax.rem(place, PIXELS)
    place = place - pixel + lax.rem(pixel, W) * H + pixel // W
    place = jnp.where(row < here, place, -1)

    scale_of = jnp.concatenate(
        [
            jnp.sum(meta_in[g * per_group : (g + 1) * per_group, 0, :], 0, keepdims=True)
            for g in range(slots // 128)
        ],
        1,
    )
    row_scale = []
    for f in range(FRAMES_HERE):
        rows = lax.broadcasted_iota(jnp.int32, (PIXELS, slots), 0) + f * PIXELS
        chosen = rows == place
        order[f] = chosen.astype(f32).astype(bf16)
        row_scale.append(jnp.sum(jnp.where(chosen, scale_of, 0.0), 1, keepdims=True))
        acc[f] = jnp.broadcast_to(res_bias_ref[...][None, :], (PIXELS, channels))
        acc[FRAMES_HERE + f] = jnp.zeros((PIXELS, channels), f32)

    gain, shift = gain_ref[...][None, :], shift_ref[...][None, :]

    def store_shifted(target, top, value):
        width = value.shape[1]
        y_index = lax.rem(lax.broadcasted_iota(jnp.int32, value.shape, 0), H)
        above = jnp.where(y_index == 0, 0.0, pltpu.roll(value, 1, 0))
        below = jnp.where(y_index == H - 1, 0.0, pltpu.roll(value, PIXELS - 1, 0))
        for a, piece in enumerate((above, value, below)):
            target[top : top + PIXELS, a * width : (a + 1) * width] = piece.astype(bf16)

    right = lax.rem(me + 1, n)

    def hop(i, own, halo):
        return pltpu.make_async_remote_copy(
            src_ref=own,
            dst_ref=halo,
            send_sem=halo_send_sem.at[i],
            recv_sem=halo_recv_sem.at[i],
            device_id={"tm": right},
            device_id_type=MESH,
        )

    hops = (
        (0, pass_out.at[1], pass_in.at[1]),
        (1, pass_out.at[0], pass_in.at[0]),
        (2, resid_own.at[1], resid_halo.at[1]),
        (3, resid_own.at[0], resid_halo.at[0]),
    )

    def send(i):
        @pl.when(me < n - 1)
        def _():
            hop(*hops[i]).start()

    def receive(i):
        @pl.when(me > 0)
        def _():
            hop(*hops[i]).wait_recv()

    def sent(i):
        @pl.when(me < n - 1)
        def _():
            hop(*hops[i]).wait_send()

    def gathered(i):
        if capacity % 16:
            return recv[i].astype(f32).reshape(slots, cut).astype(bf16)
        return recv[i].reshape(slots, cut)

    def land(i, f, arrived):
        lo, hi = i * cut, (i + 1) * cut
        values = jnp.dot(order[f], arrived, preferred_element_type=f32)
        u = values * row_scale[f] * gain[:, lo:hi] + shift[:, lo:hi]
        act = (u / (1.0 + jnp.exp(-u))).astype(bf16)
        acc[f, :, lo:hi] += values
        store_shifted(windows.at[i, f], H, act.astype(f32))

    def taps(i, j, frames):
        lo, hi = i * cut, (i + 1) * cut
        weights = jnp.concatenate([res_w[j, a, b, lo:hi] for b in range(3) for a in range(3)], 0)
        lhs = jnp.concatenate(
            [
                windows[i, frames, b * H : b * H + PIXELS, :].reshape(-1, 3 * cut)
                for b in range(3)
            ],
            1,
        )
        return jnp.dot(lhs, weights, preferred_element_type=f32)

    both = slice(0, FRAMES_HERE)
    loads[1].wait()
    for i in range(chunks - 1):
        wait_all(packed.at[i], recv.at[i], send_sem.at[i], recv_sem.at[i])
        arrived = gathered(i)
        for f in range(FRAMES_HERE):
            land(i, f, arrived)
        acc[both] += taps(i, 2, both).reshape(FRAMES_HERE, PIXELS, channels)
        middle = taps(i, 1, both)
        acc[1] += keep[1][1] * middle[:PIXELS]
        acc[2] += keep[2][1] * middle[PIXELS:]
        last = taps(i, 0, both)
        acc[2] += keep[2][0] * last[:PIXELS]
        acc[3] += keep[3][0] * last[PIXELS:]

    i = chunks - 1
    wait_all(packed.at[i], recv.at[i], send_sem.at[i], recv_sem.at[i])
    arrived = gathered(i)
    early, late = slice(0, 1), slice(1, 2)
    land(i, 1, arrived)
    pass_out[1] = (acc[3] + keep[3][0] * taps(i, 0, late)).astype(bf16)
    send(0)
    land(i, 0, arrived)
    acc[2] += keep[2][1] * taps(i, 1, late)
    pass_out[0] = (acc[2] + keep[2][0] * taps(i, 0, early)).astype(bf16)
    send(1)
    acc[1] += taps(i, 2, late)
    acc[1] += keep[1][1] * taps(i, 1, early)
    acc[0] += taps(i, 2, early)

    loads[2].wait()
    time_bias = time_bias_ref[...][None, :]

    def mix(value, j):
        return jnp.dot(value, time_w[j], preferred_element_type=f32)

    receive(0)
    resid_own[1] = (acc[1] + pass_in[1].astype(f32)).astype(bf16)
    send(2)
    temporal[1] = mix(resid_own[1], 2) + time_bias
    receive(1)
    resid_own[0] = (acc[0] + pass_in[0].astype(f32)).astype(bf16)
    send(3)
    temporal[1] += keep[1][1] * mix(resid_own[0], 1)
    temporal[0] = mix(resid_own[0], 2) + time_bias

    bias = bias_row[...]
    bias = (bias + pltpu.roll(bias, up_channels, 1))[0:1]
    edge = jnp.zeros((H, 128), f32)
    lane_index = lax.broadcasted_iota(jnp.int32, (PIXELS, 128), 1)

    def enlarge(f):
        for half in range(2):
            frame = temporal[f, :, half * channels : (half + 1) * channels]
            store_shifted(enlarged.at[2 * f + half], 0, frame.astype(bf16).astype(f32))

    def upscale(f):
        for p in range(2):
            lhs = enlarged[2 * f : 2 * f + 2, :, p * channels : (p + 2) * channels]
            product = jnp.dot(
                lhs.reshape(2 * PIXELS, 2 * channels), up_w[p], preferred_element_type=f32
            )
            for half in range(2):
                rows = slice(half * PIXELS, (half + 1) * PIXELS)
                for t in range(pair // 128):
                    same = product[rows, t * 128 : (t + 1) * 128]
                    side = product[rows, pair + t * 128 : pair + (t + 1) * 128]
                    before_it = jnp.concatenate([edge, side[: PIXELS - H]], 0)
                    after_it = jnp.concatenate([side[H:], edge], 0)
                    if (t + 1) * 128 <= up_channels:
                        moved = before_it
                    elif t * 128 >= up_channels:
                        moved = after_it
                    else:
                        moved = jnp.where(lane_index < up_channels - t * 128, before_it, after_it)
                    woven[half, t, pl.ds(p, PIXELS, stride=2), :] = (
                        same + moved + bias[:, t * 128 : (t + 1) * 128]
                    )
        for half in range(2):
            for t in range(pair // 128):
                value = woven[half, t].astype(bf16)
                for x in range(W):
                    base = x * pair + t * 128
                    out_ref[2 * f + half, :, base : base + 128] = value[
                        x * 2 * H : (x + 1) * 2 * H
                    ]

    receive(2)
    temporal[1] += keep[1][0] * mix(resid_halo[1], 0)
    enlarge(1)
    upscale(1)
    temporal[0] += keep[0][1] * mix(resid_halo[1], 1)
    receive(3)
    temporal[0] += keep[0][0] * mix(resid_halo[0], 0)
    enlarge(0)
    upscale(0)

    for i in range(len(hops)):
        sent(i)


def on_device(
    latent,
    owner,
    frame_counts,
    norm_gain,
    norm_shift,
    res_kernel,
    res_bias,
    time_kernel,
    time_bias,
    up_kernel,
    up_bias,
):
    n = lax.axis_size("tm")
    tokens, channels = latent.shape
    capacity = 2 * tokens // n
    up_channels = up_kernel.shape[-1]
    cut = 128
    chunks = channels // cut
    f32, bf16 = jnp.float32, jnp.bfloat16
    vmem = pl.BlockSpec(memory_space=pltpu.VMEM)
    smem = pl.BlockSpec(memory_space=pltpu.SMEM)
    hbm = pl.BlockSpec(memory_space=pl.ANY)
    frame = (FRAMES_HERE, PIXELS)
    return pl.pallas_call(
        functools.partial(kernel, n),
        out_shape=pltpu.VMEM((2 * FRAMES_HERE, 2 * H, 2 * W * up_channels), bf16),
        in_specs=[vmem, smem, vmem, vmem, vmem, vmem, vmem, vmem, hbm, hbm, hbm],
        out_specs=vmem,
        scratch_shapes=[
            pltpu.VMEM(res_kernel.shape, bf16),
            pltpu.VMEM(time_kernel.shape, bf16),
            pltpu.VMEM((3, 3, up_channels, channels), bf16),
            pltpu.VMEM((2, 2 * channels, 4 * up_channels), bf16),
            pltpu.VMEM((chunks, n, capacity, cut), bf16),
            pltpu.VMEM((chunks, n, capacity, cut), bf16),
            pltpu.VMEM((*frame, n * capacity), bf16),
            pltpu.VMEM((n, 1, 128), f32),
            pltpu.VMEM((n, 1, 128), f32),
            pltpu.VMEM((2 * FRAMES_HERE, PIXELS, channels), f32),
            pltpu.VMEM((*frame, channels), bf16),
            pltpu.VMEM((*frame, channels), bf16),
            pltpu.VMEM((*frame, channels), bf16),
            pltpu.VMEM((*frame, channels), bf16),
            pltpu.VMEM((chunks, FRAMES_HERE, PIXELS + 2 * H, 3 * cut), bf16),
            pltpu.VMEM((*frame, 2 * channels), f32),
            pltpu.VMEM((2 * FRAMES_HERE, PIXELS, 3 * channels), bf16),
            pltpu.VMEM((2, 2 * up_channels // 128, 2 * PIXELS, 128), f32),
            pltpu.VMEM((4 * up_channels, channels), f32),
            pltpu.VMEM((8, 2 * up_channels), f32),
            pltpu.SemaphoreType.DMA((3,)),
            pltpu.SemaphoreType.DMA((chunks,)),
            pltpu.SemaphoreType.DMA((chunks,)),
            pltpu.SemaphoreType.DMA,
            pltpu.SemaphoreType.DMA,
            pltpu.SemaphoreType.DMA((4,)),
            pltpu.SemaphoreType.DMA((4,)),
        ],
        compiler_params=pltpu.CompilerParams(
            collective_id=0, has_side_effects=True, vmem_limit_bytes=60 << 20
        ),
    )(
        owner.reshape(1, tokens),
        frame_counts,
        latent,
        norm_gain,
        norm_shift,
        res_bias,
        time_bias,
        up_bias,
        res_kernel,
        time_kernel,
        up_kernel.swapaxes(2, 3),
    )


def solution(mesh):
    placed = (
        P(("groups", "tm"), None),
        P(("groups", "tm")),
        P("groups"),
        P(),
        P(),
        P(),
        P(),
        P(),
        P(),
        P(),
        P(),
    )
    return jax.shard_map(
        on_device,
        mesh=mesh,
        in_specs=placed,
        out_specs=P(("groups", "tm"), None, None),
        check_vma=False,
    )
```

time: 45.6 us -> 38.2 us (0.84)
  Pallas kernels: 44.3 us -> 36.9 us
    pallas_call x1, Pallas kernels: 44.3 us -> 36.9 us  [on_device(): pl.pallas_call(functools.partial(kernel, n), out_shape=pltpu.VMEM((2 * FR...]
where the time goes in v1:
time: 38.2 us; the launch traced here: 38 us
  Pallas kernels  36.9 us (97%)
  local copies, waits for them, and re-layouts  1.15 us (3%)
    pallas_call x1, Pallas kernels, on_device(): pl.pallas_call(functools.partial(kernel, n), out_shape=pltpu.VMEM((2 * FR...  36.9 us
    unnamed x1, local copies, waits for them, and re-layouts  1.15 us

profile of v1, /device:TPU:16, one launch (start us, length us, event | category | flops | bytes accessed | tf_op | source)
XLA Modules:
  0.0 38.0 jit_solution(4197230950780418779)
XLA Ops:
  0.0 36.9 %shard_map.109 = bf16[4,32,6144]{2,1,0:T(8,128)(2,1)S(1)} custom-call(s32[1,512]{1,0:T(1,128)} %bitcast.3, s32[8]{0:T(128)} %counts_ref.1, bf16[512,384]{1,0:T(8,128)(2,1)} %latent_ref.1, f32[384]{0:T(512)} %gain_ref.1, f32[384]{0:T(512)} %shift_ref.1, f32[384]{0:T(512)} %res_bias_ref.1, f32[768]{0:T(1024)} %time_bias_ref.1, f32[192]{0:T(256)} %up_bias_ref.1, ...), custom_call_target="tpu_custom_call" | custom-call | tf_op jit(solution)/shard_map/pallas_call | solution.py:435
  36.9 1.1 %copy.13 = bf16[4,32,6144]{2,1,0:T(8,128)(2,1)} copy(bf16[4,32,6144]{2,1,0:T(8,128)(2,1)S(1)} %shard_map.109) | data formatting | bytes 3145728

commit v2 on v1

--- a/solution.py
+++ b/solution.py
@@ -41,11 +41,12 @@
     meta_out,
     meta_in,
     acc,
-    pass_out,
-    pass_in,
+    act_own,
+    act_halo,
     resid_own,
     resid_halo,
     windows,
+    halo_windows,
     temporal,
     enlarged,
     woven,
@@ -160,10 +161,12 @@
         for f in range(FRAMES_HERE):
             windows[i, f, 0:H] = border
             windows[i, f, H + PIXELS : 2 * H + PIXELS] = border
+            halo_windows[i, f, 0:H] = border
+            halo_windows[i, f, H + PIXELS : 2 * H + PIXELS] = border
 
     @pl.when(me == 0)
     def _():
-        pass_in[...] = jnp.zeros_like(pass_in)
+        act_halo[...] = jnp.zeros_like(act_halo)
         resid_halo[...] = jnp.zeros_like(resid_halo)
 
     bias_row[...] = jnp.zeros_like(bias_row)
@@ -187,7 +190,7 @@
 
     first = me * FRAMES_HERE
     keep = []
-    for f in range(2 * FRAMES_HERE):
+    for f in range(FRAMES_HERE):
         start = jnp.int32(0)
         begin = jnp.int32(0)
         for v in range(counts_ref.shape[0]):
@@ -236,7 +239,6 @@
         order[f] = chosen.astype(f32).astype(bf16)
         row_scale.append(jnp.sum(jnp.where(chosen, scale_of, 0.0), 1, keepdims=True))
         acc[f] = jnp.broadcast_to(res_bias_ref[...][None, :], (PIXELS, channels))
-        acc[FRAMES_HERE + f] = jnp.zeros((PIXELS, channels), f32)
 
     gain, shift = gain_ref[...][None, :], shift_ref[...][None, :]
 
@@ -260,27 +262,26 @@
             device_id_type=MESH,
         )
 
-    hops = (
-        (0, pass_out.at[1], pass_in.at[1]),
-        (1, pass_out.at[0], pass_in.at[0]),
-        (2, resid_own.at[1], resid_halo.at[1]),
-        (3, resid_own.at[0], resid_halo.at[0]),
-    )
+    hops = [(act_own.at[i], act_halo.at[i]) for i in range(chunks - 1)]
+    for owned, halo in ((act_own.at[chunks - 1], act_halo.at[chunks - 1]), (resid_own, resid_halo)):
+        hops += [(owned.at[1], halo.at[1]), (owned.at[0], halo.at[0])]
+    last = chunks - 1
+    resid = chunks + 1
 
     def send(i):
         @pl.when(me < n - 1)
         def _():
-            hop(*hops[i]).start()
+            hop(i, *hops[i]).start()
 
     def receive(i):
         @pl.when(me > 0)
         def _():
-            hop(*hops[i]).wait_recv()
+            hop(i, *hops[i]).wait_recv()
 
     def sent(i):
         @pl.when(me < n - 1)
         def _():
-            hop(*hops[i]).wait_send()
+            hop(i, *hops[i]).wait_send()
 
     def gathered(i):
         if capacity % 16:
@@ -293,49 +294,68 @@
         u = values * row_scale[f] * gain[:, lo:hi] + shift[:, lo:hi]
         act = (u / (1.0 + jnp.exp(-u))).astype(bf16)
         acc[f, :, lo:hi] += values
-        store_shifted(windows.at[i, f], H, act.astype(f32))
-
-    def taps(i, j, frames):
+        act_own[i, f] = act
+        return act.astype(f32)
+
+    def spread(i, f, act):
+        store_shifted(windows.at[i, f], H, act)
+
+    def taps(i, j, frames, source=windows):
         lo, hi = i * cut, (i + 1) * cut
         weights = jnp.concatenate([res_w[j, a, b, lo:hi] for b in range(3) for a in range(3)], 0)
         lhs = jnp.concatenate(
             [
-                windows[i, frames, b * H : b * H + PIXELS, :].reshape(-1, 3 * cut)
+                source[i, frames, b * H : b * H + PIXELS, :].reshape(-1, 3 * cut)
                 for b in range(3)
             ],
             1,
         )
         return jnp.dot(lhs, weights, preferred_element_type=f32)
 
-    both = slice(0, FRAMES_HERE)
+    both, early, late = slice(0, FRAMES_HERE), slice(0, 1), slice(1, 2)
+
+    def own_taps(i):
+        acc[...] += taps(i, 2, both).reshape(FRAMES_HERE, PIXELS, channels)
+        acc[1] += keep[1][1] * taps(i, 1, early)
+
+    def halo_taps():
+        for i in range(chunks - 1):
+            receive(i)
+            for f in range(FRAMES_HERE):
+                store_shifted(halo_windows.at[i, f], H, act_halo[i, f].astype(f32))
+            oldest = taps(i, 0, both, halo_windows)
+            acc[0] += keep[0][0] * oldest[:PIXELS]
+            acc[1] += keep[1][0] * oldest[PIXELS:]
+            acc[0] += keep[0][1] * taps(i, 1, late, halo_windows)
+
+    paired = lax.rem(me, 2) == 1
     loads[1].wait()
     for i in range(chunks - 1):
         wait_all(packed.at[i], recv.at[i], send_sem.at[i], recv_sem.at[i])
         arrived = gathered(i)
+        acts = [land(i, f, arrived) for f in range(FRAMES_HERE)]
+        send(i)
         for f in range(FRAMES_HERE):
-            land(i, f, arrived)
-        acc[both] += taps(i, 2, both).reshape(FRAMES_HERE, PIXELS, channels)
-        middle = taps(i, 1, both)
-        acc[1] += keep[1][1] * middle[:PIXELS]
-        acc[2] += keep[2][1] * middle[PIXELS:]
-        last = taps(i, 0, both)
-        acc[2] += keep[2][0] * last[:PIXELS]
-        acc[3] += keep[3][0] * last[PIXELS:]
-
-    i = chunks - 1
-    wait_all(packed.at[i], recv.at[i], send_sem.at[i], recv_sem.at[i])
-    arrived = gathered(i)
-    early, late = slice(0, 1), slice(1, 2)
-    land(i, 1, arrived)
-    pass_out[1] = (acc[3] + keep[3][0] * taps(i, 0, late)).astype(bf16)
-    send(0)
-    land(i, 0, arrived)
-    acc[2] += keep[2][1] * taps(i, 1, late)
-    pass_out[0] = (acc[2] + keep[2][0] * taps(i, 0, early)).astype(bf16)
-    send(1)
-    acc[1] += taps(i, 2, late)
-    acc[1] += keep[1][1] * taps(i, 1, early)
-    acc[0] += taps(i, 2, early)
+            spread(i, f, acts[f])
+        own_taps(i)
+
+    @pl.when(paired)
+    def _():
+        halo_taps()
+
+    wait_all(packed.at[last], recv.at[last], send_sem.at[last], recv_sem.at[last])
+    arrived = gathered(last)
+    acts = {}
+    for f in (1, 0):
+        acts[f] = land(last, f, arrived)
+        send(last + 1 - f)
+    for f in (1, 0):
+        spread(last, f, acts[f])
+    own_taps(last)
+
+    @pl.when(jnp.logical_not(paired))
+    def _():
+        halo_taps()
 
     loads[2].wait()
     time_bias = time_bias_ref[...][None, :]
@@ -343,13 +363,16 @@
     def mix(value, j):
         return jnp.dot(value, time_w[j], preferred_element_type=f32)
 
-    receive(0)
-    resid_own[1] = (acc[1] + pass_in[1].astype(f32)).astype(bf16)
-    send(2)
+    receive(last)
+    store_shifted(halo_windows.at[last, 1], H, act_halo[last, 1].astype(f32))
+    resid_own[1] = (acc[1] + keep[1][0] * taps(last, 0, late, halo_windows)).astype(bf16)
+    send(resid)
+    acc[0] += keep[0][1] * taps(last, 1, late, halo_windows)
+    receive(last + 1)
+    store_shifted(halo_windows.at[last, 0], H, act_halo[last, 0].astype(f32))
+    resid_own[0] = (acc[0] + keep[0][0] * taps(last, 0, early, halo_windows)).astype(bf16)
+    send(resid + 1)
     temporal[1] = mix(resid_own[1], 2) + time_bias
-    receive(1)
-    resid_own[0] = (acc[0] + pass_in[0].astype(f32)).astype(bf16)
-    send(3)
     temporal[1] += keep[1][1] * mix(resid_own[0], 1)
     temporal[0] = mix(resid_own[0], 2) + time_bias
 
@@ -394,12 +417,12 @@
                         x * 2 * H : (x + 1) * 2 * H
                     ]
 
-    receive(2)
+    receive(resid)
     temporal[1] += keep[1][0] * mix(resid_halo[1], 0)
     enlarge(1)
     upscale(1)
     temporal[0] += keep[0][1] * mix(resid_halo[1], 1)
-    receive(3)
+    receive(resid + 1)
     temporal[0] += keep[0][0] * mix(resid_halo[0], 0)
     enlarge(0)
     upscale(0)
@@ -447,11 +470,12 @@
             pltpu.VMEM((*frame, n * capacity), bf16),
             pltpu.VMEM((n, 1, 128), f32),
             pltpu.VMEM((n, 1, 128), f32),
-            pltpu.VMEM((2 * FRAMES_HERE, PIXELS, channels), f32),
+            pltpu.VMEM((*frame, channels), f32),
+            pltpu.VMEM((chunks, *frame, cut), bf16),
+            pltpu.VMEM((chunks, *frame, cut), bf16),
             pltpu.VMEM((*frame, channels), bf16),
             pltpu.VMEM((*frame, channels), bf16),
-            pltpu.VMEM((*frame, channels), bf16),
-            pltpu.VMEM((*frame, channels), bf16),
+            pltpu.VMEM((chunks, FRAMES_HERE, PIXELS + 2 * H, 3 * cut), bf16),
             pltpu.VMEM((chunks, FRAMES_HERE, PIXELS + 2 * H, 3 * cut), bf16),
             pltpu.VMEM((*frame, 2 * channels), f32),
             pltpu.VMEM((2 * FRAMES_HERE, PIXELS, 3 * channels), bf16),
@@ -463,8 +487,8 @@
             pltpu.SemaphoreType.DMA((chunks,)),
             pltpu.SemaphoreType.DMA,
             pltpu.SemaphoreType.DMA,
-            pltpu.SemaphoreType.DMA((4,)),
-            pltpu.SemaphoreType.DMA((4,)),
+            pltpu.SemaphoreType.DMA((chunks + 3,)),
+            pltpu.SemaphoreType.DMA((chunks + 3,)),
         ],
         compiler_params=pltpu.CompilerParams(
             collective_id=0, has_side_effects=True, vmem_limit_bytes=60 << 20

time: 38.2 us -> 37 us (0.969)
  Pallas kernels: 36.9 us -> 35.7 us
    pallas_call x1, Pallas kernels: 36.9 us -> 35.7 us  [on_device(): pl.pallas_call(functools.partial(kernel, n), out_shape=pltpu.VMEM((2 * FR...]
where the time goes in v2:
time: 37 us; the launch traced here: 36.8 us
  Pallas kernels  35.7 us (96%)
  local copies, waits for them, and re-layouts  1.15 us (3%)
    pallas_call x1, Pallas kernels, on_device(): pl.pallas_call(functools.partial(kernel, n), out_shape=pltpu.VMEM((2 * FR...  35.7 us
    unnamed x1, local copies, waits for them, and re-layouts  1.15 us

profile of v2, /device:TPU:16, one launch (start us, length us, event | category | flops | bytes accessed | tf_op | source)
XLA Modules:
  0.0 36.8 jit_solution(4855493142193510622)
XLA Ops:
  0.0 35.7 %shard_map.109 = bf16[4,32,6144]{2,1,0:T(8,128)(2,1)S(1)} custom-call(s32[1,512]{1,0:T(1,128)} %bitcast.3, s32[8]{0:T(128)} %counts_ref.1, bf16[512,384]{1,0:T(8,128)(2,1)} %latent_ref.1, f32[384]{0:T(512)} %gain_ref.1, f32[384]{0:T(512)} %shift_ref.1, f32[384]{0:T(512)} %res_bias_ref.1, f32[768]{0:T(1024)} %time_bias_ref.1, f32[192]{0:T(256)} %up_bias_ref.1, ...), custom_call_target="tpu_custom_call" | custom-call | tf_op jit(solution)/shard_map/pallas_call | solution.py:458
  35.7 1.1 %copy.13 = bf16[4,32,6144]{2,1,0:T(8,128)(2,1)} copy(bf16[4,32,6144]{2,1,0:T(8,128)(2,1)S(1)} %shard_map.109) | data formatting | bytes 3145728

commit v3 on v2

--- a/solution.py
+++ b/solution.py
@@ -59,6 +59,7 @@
     meta_recv_sem,
     halo_send_sem,
     halo_recv_sem,
+    known_sem,
 ):
     me = lax.axis_index("tm")
     tokens, channels = latent_ref.shape
@@ -70,11 +71,19 @@
 
     barrier = pltpu.get_barrier_semaphore()
 
-    @pl.loop(1, n)
-    def _(k):
+    bits = [1 << b for b in range(n.bit_length() - 1)]
+    assert n == 1 << len(bits)
+
+    def partner(k):
+        return me + sum(b * (1 - 2 * lax.rem(me // b, 2)) for b in bits if k & b)
+
+    def greet(semaphore, k):
         pl.semaphore_signal(
-            barrier, inc=1, device_id={"tm": lax.rem(me + k, n)}, device_id_type=MESH
+            semaphore, inc=1, device_id={"tm": partner(k)}, device_id_type=MESH
         )
+
+    for b in bits:
+        greet(barrier, b)
 
     loads = [
         pltpu.make_async_copy(src, dst, load_sem.at[i])
@@ -125,32 +134,45 @@
                 block[:, i * cut : (i + 1) * cut].reshape(per, capacity, cut).astype(bf16)
             )
 
-    pl.semaphore_wait(barrier, n - 1)
-
-    @pl.loop(1, n)
-    def _(k):
-        peer = lax.rem(me + k, n)
+    pl.semaphore_wait(barrier, len(bits))
+
+    def post(i, peer):
         pltpu.make_async_remote_copy(
-            src_ref=meta_out.at[k],
-            dst_ref=meta_in.at[me],
-            send_sem=meta_send_sem,
-            recv_sem=meta_recv_sem,
+            src_ref=packed.at[i, lax.rem(peer - me + n, n)],
+            dst_ref=recv.at[i, me],
+            send_sem=send_sem.at[i],
+            recv_sem=recv_sem.at[i],
             device_id={"tm": peer},
             device_id_type=MESH,
         ).start()
 
-    for i in range(chunks):
+    def open_with(offsets):
+        for k in sorted(offsets, reverse=True):
+            peer = partner(k)
+            pltpu.make_async_remote_copy(
+                src_ref=meta_out.at[lax.rem(peer - me + n, n)],
+                dst_ref=meta_in.at[me],
+                send_sem=meta_send_sem,
+                recv_sem=meta_recv_sem,
+                device_id={"tm": peer},
+                device_id_type=MESH,
+            ).start()
+            post(0, peer)
+
+    known = set(bits)
+    for r, b in enumerate(bits[:-1]):
+        greet(known_sem.at[r], b)
+        open_with(known if r == 0 else known - older)
+        older = set(known)
+        known |= {b ^ k for k in known if k != b}
+        pl.semaphore_wait(known_sem.at[r], 1)
+    open_with(known - older)
+
+    for i in range(1, chunks):
 
         @pl.loop(1, n)
         def _(k):
-            pltpu.make_async_remote_copy(
-                src_ref=packed.at[i, k],
-                dst_ref=recv.at[i, me],
-                send_sem=send_sem.at[i],
-                recv_sem=recv_sem.at[i],
-                device_id={"tm": lax.rem(me + k, n)},
-                device_id_type=MESH,
-            ).start()
+            post(i, lax.rem(me + k, n))
 
     meta_in[me] = meta_out[0]
     for i in range(chunks):
@@ -489,6 +511,7 @@
             pltpu.SemaphoreType.DMA,
             pltpu.SemaphoreType.DMA((chunks + 3,)),
             pltpu.SemaphoreType.DMA((chunks + 3,)),
+            pltpu.SemaphoreType.REGULAR((max(n.bit_length() - 2, 1),)),
         ],
         compiler_params=pltpu.CompilerParams(
             collective_id=0, has_side_effects=True, vmem_limit_bytes=60 << 20

time: 37 us -> 36.6 us (0.989)
  Pallas kernels: 35.7 us -> 35.3 us
    pallas_call x1, Pallas kernels: 35.7 us -> 35.3 us  [on_device(): pl.pallas_call(functools.partial(kernel, n), out_shape=pltpu.VMEM((2 * FR...]
where the time goes in v3:
time: 36.6 us; the launch traced here: 36.4 us
  Pallas kernels  35.3 us (96%)
  local copies, waits for them, and re-layouts  1.15 us (3%)
    pallas_call x1, Pallas kernels, on_device(): pl.pallas_call(functools.partial(kernel, n), out_shape=pltpu.VMEM((2 * FR...  35.3 us
    unnamed x1, local copies, waits for them, and re-layouts  1.15 us

profile of v3, /device:TPU:16, one launch (start us, length us, event | category | flops | bytes accessed | tf_op | source)
XLA Modules:
  0.0 36.4 jit_solution(7092736334874262829)
XLA Ops:
  0.0 35.3 %shard_map.109 = bf16[4,32,6144]{2,1,0:T(8,128)(2,1)S(1)} custom-call(s32[1,512]{1,0:T(1,128)} %bitcast.3, s32[8]{0:T(128)} %counts_ref.1, bf16[512,384]{1,0:T(8,128)(2,1)} %latent_ref.1, f32[384]{0:T(512)} %gain_ref.1, f32[384]{0:T(512)} %shift_ref.1, f32[384]{0:T(512)} %res_bias_ref.1, f32[768]{0:T(1024)} %time_bias_ref.1, f32[192]{0:T(256)} %up_bias_ref.1, ...), custom_call_target="tpu_custom_call" | custom-call | tf_op jit(solution)/shard_map/pallas_call | solution.py:480
  35.3 1.1 %copy.13 = bf16[4,32,6144]{2,1,0:T(8,128)(2,1)} copy(bf16[4,32,6144]{2,1,0:T(8,128)(2,1)S(1)} %shard_map.109) | data formatting | bytes 3145728

commit v4 on v3

--- a/solution.py
+++ b/solution.py
@@ -373,7 +373,8 @@
         send(last + 1 - f)
     for f in (1, 0):
         spread(last, f, acts[f])
-    own_taps(last)
+    acc[1] += taps(last, 2, late)
+    acc[1] += keep[1][1] * taps(last, 1, early)
 
     @pl.when(jnp.logical_not(paired))
     def _():
@@ -389,6 +390,7 @@
     store_shifted(halo_windows.at[last, 1], H, act_halo[last, 1].astype(f32))
     resid_own[1] = (acc[1] + keep[1][0] * taps(last, 0, late, halo_windows)).astype(bf16)
     send(resid)
+    acc[0] += taps(last, 2, early)
     acc[0] += keep[0][1] * taps(last, 1, late, halo_windows)
     receive(last + 1)
     store_shifted(halo_windows.at[last, 0], H, act_halo[last, 0].astype(f32))

time: 36.6 us -> 36.2 us (0.989)
  Pallas kernels: 35.3 us -> 34.9 us
    pallas_call x1, Pallas kernels: 35.3 us -> 34.9 us  [on_device(): pl.pallas_call(functools.partial(kernel, n), out_shape=pltpu.VMEM((2 * FR...]
where the time goes in v4:
time: 36.2 us; the launch traced here: 36 us
  Pallas kernels  34.9 us (96%)
  local copies, waits for them, and re-layouts  1.15 us (3%)
    pallas_call x1, Pallas kernels, on_device(): pl.pallas_call(functools.partial(kernel, n), out_shape=pltpu.VMEM((2 * FR...  34.9 us
    unnamed x1, local copies, waits for them, and re-layouts  1.15 us

profile of v4, /device:TPU:16, one launch (start us, length us, event | category | flops | bytes accessed | tf_op | source)
XLA Modules:
  0.0 36.0 jit_solution(4059484862949670956)
XLA Ops:
  0.0 34.9 %shard_map.109 = bf16[4,32,6144]{2,1,0:T(8,128)(2,1)S(1)} custom-call(s32[1,512]{1,0:T(1,128)} %bitcast.3, s32[8]{0:T(128)} %counts_ref.1, bf16[512,384]{1,0:T(8,128)(2,1)} %latent_ref.1, f32[384]{0:T(512)} %gain_ref.1, f32[384]{0:T(512)} %shift_ref.1, f32[384]{0:T(512)} %res_bias_ref.1, f32[768]{0:T(1024)} %time_bias_ref.1, f32[192]{0:T(256)} %up_bias_ref.1, ...), custom_call_target="tpu_custom_call" | custom-call | tf_op jit(solution)/shard_map/pallas_call | solution.py:482
  34.9 1.1 %copy.13 = bf16[4,32,6144]{2,1,0:T(8,128)(2,1)} copy(bf16[4,32,6144]{2,1,0:T(8,128)(2,1)S(1)} %shard_map.109) | data formatting | bytes 3145728
